TPU v7x, 32 devices: a whole 2x2x4 slice. The times are simulated.
32 devices in a mesh: dp: 4 (over y, x), fsdp: 4 (over z), crop: 2 (over core).
Axes of the slice: x: 2, y: 2, z: 4, core: 2. Of those that a mesh axis runs over, the one named last changes fastest.
Arguments:
- grad_parts: float32 [8, 848, 1536], P(('dp', 'crop'), None, 'fsdp'), may hold values from -1.5 to 1.5
- student: float32 [848, 1536], P(('dp', 'crop'), 'fsdp'), may hold values from -2 to 2
- teacher: float32 [848, 1536], P(('dp', 'crop'), 'fsdp'), may hold values from -2 to 2
- moment1: float32 [848, 1536], P(('dp', 'crop'), 'fsdp'), may hold values from -0.6 to 0.6
- moment2: float32 [848, 1536], P(('dp', 'crop'), 'fsdp'), may hold values from 0.001 to 0.01
- step_count: int32 [1], replicated, may hold values from 1 to 1999
- pixels: bfloat16 [16, 2, 256, 588], P(('dp', 'fsdp'), 'crop'), may hold values from -5 to 5
- assign: int32 [16, 2], P(('dp', 'fsdp')), may hold values from 0 to 1, each once within a row
Outputs:
- student_new: float32 [848, 1536], P(('dp', 'crop'), 'fsdp')
- moment1_new: float32 [848, 1536], P(('dp', 'crop'), 'fsdp')
- moment2_new: float32 [848, 1536], P(('dp', 'crop'), 'fsdp')
- teacher_new: float32 [848, 1536], P(('dp', 'crop'), 'fsdp')
- student_step: float32 [848, 1536], P(('dp', 'crop'), 'fsdp')
- teacher_tokens: float32 [16, 2, 257, 1536], P(('dp', 'fsdp'))
Inputs may be any that keep to these rules, and one draw needn't show every extreme that they name: `assign`: each row holds 0 and 1 once.
All inputs are finite; a program needn't handle non-finite values.
Results may differ from a plain program's by a relative error of at most 0.0003.
Values may be sent and summed in bfloat16 or wider, within the bound.
A program may use at most 64 MiB of HBM per device.

v0:
```python
import math

import jax
import jax.numpy as jnp
from jax import lax
from jax.sharding import PartitionSpec as P

beta_one = 0.9
beta_two = 0.999
adam_epsilon = 1e-08
learn_rate = 0.001
weight_decay = 0.04
momentum_base = 0.992
plan_length = 625000.0
norm_epsilon = 1e-06


def optimize(gradient, student, teacher, moment1, moment2, step_count):
    step_value = step_count[0].astype(jnp.float32)
    first_moment = beta_one * moment1 + (1.0 - beta_one) * gradient
    second_moment = beta_two * moment2 + (1.0 - beta_two) * gradient * gradient
    first_fix = 1.0 - jnp.power(jnp.float32(beta_one), step_value)
    second_fix = 1.0 - jnp.power(jnp.float32(beta_two), step_value)
    update = (
        first_moment / first_fix / (jnp.sqrt(second_moment / second_fix) + adam_epsilon)
        + weight_decay * student
    )
    student_new = student - learn_rate * update
    momentum = (
        1.0 - (1.0 - momentum_base) * (jnp.cos(math.pi * step_value / plan_length) + 1.0) / 2.0
    )
    teacher_new = momentum * teacher + (1.0 - momentum) * student_new
    return (student_new, first_moment, second_moment, teacher_new, update)


def embed(patches, table):
    count = patches.shape[0]
    pix_size = patches.shape[2]
    patch_count = patches.shape[1]
    width = table.shape[1]
    weight = table[:pix_size]
    position = table[pix_size : pix_size + patch_count]
    extras = table[pix_size + patch_count :]
    flat_patches = patches.reshape(count * patch_count, pix_size).astype(jnp.float32)
    projected = jnp.dot(
        flat_patches, weight, precision=lax.Precision.HIGHEST, preferred_element_type=jnp.float32
    )
    projected = projected.reshape(count, patch_count, width) + extras[1] + position
    class_row = jnp.broadcast_to(extras[0], (count, 1, width))
    tokens = jnp.concatenate([class_row, projected], axis=1)
    average = jnp.mean(tokens, axis=-1, keepdims=True)
    centered = tokens - average
    variance = jnp.mean(centered * centered, axis=-1, keepdims=True)
    return centered * lax.rsqrt(variance + norm_epsilon) * extras[2] + extras[3]


def shards(grad_parts, student, teacher, moment1, moment2, step_count, pixels, assign):
    gradient = lax.psum_scatter(grad_parts[0], ("dp", "crop"), scatter_dimension=0, tiled=True)
    student_new, first_moment, second_moment, teacher_new, update = optimize(
        gradient, student, teacher, moment1, moment2, step_count
    )
    column_block = lax.all_gather(teacher_new, "fsdp", axis=1, tiled=True)
    gathered = lax.all_gather(column_block, ("dp", "crop"), axis=0, tiled=True)
    own_tokens = embed(pixels[:, 0], gathered)
    both = lax.all_gather(own_tokens[:, None], "crop", axis=1, tiled=True)
    teacher_tokens = jnp.where((assign == 0)[:, :, None, None], both[:, 0:1], both[:, 1:2])
    return (student_new, first_moment, second_moment, teacher_new, update, teacher_tokens)


def solution(mesh):
    placed = (
        P(("dp", "crop"), None, "fsdp"),
        P(("dp", "crop"), "fsdp"),
        P(("dp", "crop"), "fsdp"),
        P(("dp", "crop"), "fsdp"),
        P(("dp", "crop"), "fsdp"),
        P(),
        P(("dp", "fsdp"), "crop", None, None),
        P(("dp", "fsdp"), None),
    )
    return jax.shard_map(
        shards,
        mesh=mesh,
        in_specs=placed,
        out_specs=(
            P(("dp", "crop"), "fsdp"),
            P(("dp", "crop"), "fsdp"),
            P(("dp", "crop"), "fsdp"),
            P(("dp", "crop"), "fsdp"),
            P(("dp", "crop"), "fsdp"),
            P(("dp", "fsdp"), None, None, None),
        ),
        check_vma=False,
    )
```

profile of v0, /device:TPU:9, one launch (start us, length us, event | category | flops | bytes accessed | tf_op | source)
XLA Modules:
  0.0 137.1 jit_solution(8425231990737697508)
XLA Ops:
  7.2 0.0 copy-start
  7.2 0.0 copy-start.6
  7.2 0.0 copy-start.2
  7.2 0.0 copy-start.5
  7.2 0.0 copy-start.4
  7.2 0.0 copy-start.3
  7.2 0.0 all-gather.6.cloned.1.call-start
  7.3 20.4 %fusion = f32[112,384]{1,0:T(8,128)S(1)} fusion(f32[848,384]{1,0:T(8,128)} %bitcast.31), kind=kCustom, calls=%all-reduce-scatter | all-reduce-scatter fusion | flops 344065 | bytes 1475072
  27.7 3.2 %collective-permute-start = (f32[42,384]{1,0:T(8,128)S(1)}, f32[42,384]{1,0:T(8,128)S(1)}, u32[]{:S(2)}, u32[]{:S(2)}) collective-permute-start(f32[42,384]{1,0:T(8,128)S(1)} %slice.45), channel_id=1, source_target_pairs={{0,1},{1,8},{8,9},{9,16},{16,17},{17,24},{24,25},{2,3},{3,10},{10,... | collective-permute-start | bytes 193544
  31.8 0.0 copy-done.6
  31.8 0.6 dynamic-slice.4
  33.0 0.0 collective-permute-done
  33.0 0.3 concatenate.29
  33.3 0.0 copy-done.2
  33.3 0.0 copy-done.5
  33.3 0.0 copy-done.4
  33.3 0.0 copy-done.3
  33.4 0.9 multiply_add_fusion
  34.3 0.0 copy-start.1
  34.3 15.2 %all_gather.9 = f32[106,1536]{1,0:T(8,128)} all-gather(f32[106,384]{1,0:T(8,128)S(1)} %get-tuple-element.9), channel_id=1, replica_groups=mesh['dp'=4,'fsdp'=4,'crop'=2] {'fsdp'}, dimensions={1}, use_global_device_ids=true | all-gather | bytes 814080 | tf_op jit(solution)/shard_map/all_gather | solution.py:62
  49.5 0.0 all-gather.6.cloned.1.call-update
  49.6 0.0 all-gather.4.cloned.1.call-start
  49.6 46.3 %all-gather.6.cloned.1.call-done = f32[8,106,1536]{2,1,0:T(8,128)} async-done(((f32[1,106,1536]{2,1,0:T(8,128)}), f32[8,106,1536]{2,1,0:T(8,128)}) %all-gather.6.cloned.1.call-update) | async-done | bytes 5210128 | tf_op jit(solution)/shard_map/all_gather | solution.py:63
  95.9 4.5 %reshape.278 = f32[848,1536]{1,0:T(8,128)} reshape(f32[8,106,1536]{2,1,0:T(8,128)} %all-gather.6.cloned.1.call-done) | data formatting | bytes 10420224
  100.4 0.0 copy-done.1
  100.4 1.0 slice_reduce_fusion.1
  101.4 0.0 copy-done
  101.4 4.9 %fusion.9 = f32[256,1536]{1,0:T(8,128)S(1)} fusion(f32[848,1536]{1,0:T(8,128)} %reshape.278, f32[1536]{0:T(1024)S(1)} %get-tuple-element.8, bf16[1,1,256,588]{2,3,1,0:T(8,128)(2,1)S(1)} %copy-done), kind=kOutput, calls=%fused_computation.5 | convolution fusion | flops 2775318528 | bytes 7090176 | tf_op jit(solution)/shard_map/dot_general | solution.py:45
  106.3 0.3 fusion.15
  106.5 0.5 multiply_reduce_fusion
  107.0 0.4 fusion.14
  107.4 0.0 copy-start.7
  107.4 2.8 %copy.14 = f32[1,1,257,1536]{3,0,2,1:T(1,128)} copy(f32[1,1,257,1536]{3,2,1,0:T(8,128)S(1)} %fusion.14) | data formatting | bytes 3158016 | tf_op jit(solution)/shard_map/add | solution.py:54
  110.2 0.0 all-gather.4.cloned.1.call-update
  110.2 0.0 copy-done.7
  110.2 12.6 %all-gather.4.cloned.1.call-done = f32[1,2,257,1536]{3,0,2,1:T(1,128)} async-done(((f32[1,1,257,1536]{3,0,2,1:T(1,128)}), f32[1,2,257,1536]{3,0,2,1:T(1,128)}) %all-gather.4.cloned.1.call-update) | async-done | bytes 3158032 | tf_op jit(solution)/shard_map/all_gather | solution.py:65
  122.8 4.0 %fusion.19 = (f32[1,1,257,1536]{3,0,2,1:T(1,128)S(1)}, f32[1,1,257,1536]{3,0,2,1:T(1,128)S(1)}) fusion(f32[1,2,257,1536]{3,0,2,1:T(1,128)} %all-gather.4.cloned.1.call-done), kind=kLoop, calls=%fused_computation.30 | loop fusion | bytes 6316032 | tf_op jit(solution)/shard_map/slice | solution.py:66
  126.8 0.2 copy_bitcast_fusion
  127.1 3.2 %broadcast_select_fusion = f32[1,2,257,1536]{3,1,2,0:T(2,128)} fusion(pred[2]{0:T(512)(128)(4,1)S(1)} %compare_bitcast_fusion, f32[257,1536]{1,0:T(8,128)S(1)} %get-tuple-element.18, f32[257,1536]{1,0:T(8,128)S(1)} %get-tuple-element.19), kind=kLoop, calls=%fused_computation.2 | loop fusion | flops 789504 | bytes 6316034 | tf_op jit(solution)/shard_map/jit(_where)/select_n | solution.py:66
  (4 shorter events, 0.0 us)
Async XLA Ops:
  7.2 94.2 %copy-start = (bf16[1,1,256,588]{2,3,1,0:T(8,128)(2,1)S(1)}, bf16[1,1,256,588]{2,3,1,0:T(8,128)(2,1)}, u32[]{:S(2)}) copy-start(bf16[1,1,256,588]{2,3,1,0:T(8,128)(2,1)} %param.14) | copy-start | bytes 903172
  7.2 24.6 %copy-start.6 = (u32[32]{0:T(128)S(1)}, u32[32]{0:T(128)}, u32[]{:S(2)}) copy-start(u32[32]{0:T(128)} %constant.56) | copy-start | bytes 388
  7.2 26.1 %copy-start.2 = (f32[106,384]{1,0:T(8,128)S(1)}, f32[106,384]{1,0:T(8,128)}, u32[]{:S(2)}) copy-start(f32[106,384]{1,0:T(8,128)} %param.10) | copy-start | bytes 488452
  7.2 26.1 %copy-start.5 = (f32[106,384]{1,0:T(8,128)S(1)}, f32[106,384]{1,0:T(8,128)}, u32[]{:S(2)}) copy-start(f32[106,384]{1,0:T(8,128)} %param.11) | copy-start | bytes 488452
  7.2 26.1 %copy-start.4 = (f32[106,384]{1,0:T(8,128)S(1)}, f32[106,384]{1,0:T(8,128)}, u32[]{:S(2)}) copy-start(f32[106,384]{1,0:T(8,128)} %param.12) | copy-start | bytes 488452
  7.2 26.1 %copy-start.3 = (f32[106,384]{1,0:T(8,128)S(1)}, f32[106,384]{1,0:T(8,128)}, u32[]{:S(2)}) copy-start(f32[106,384]{1,0:T(8,128)} %param.9) | copy-start | bytes 488452
  7.2 88.7 %all-gather.6.cloned.1.call-start = ((), (), s32[]{:S(2)}) async-start(), calls=%async_computation.1 | async-start | bytes 6193152 | tf_op jit(solution)/shard_map/all_gather | solution.py:63
  27.7 5.3 %collective-permute-start = (f32[42,384]{1,0:T(8,128)S(1)}, f32[42,384]{1,0:T(8,128)S(1)}, u32[]{:S(2)}, u32[]{:S(2)}) collective-permute-start(f32[42,384]{1,0:T(8,128)S(1)} %slice.45), channel_id=1, source_target_pairs={{0,1},{1,8},{8,9},{9,16},{16,17},{17,24},{24,25},{2,3},{3,10},{10,... | collective-permute-start | bytes 193544
  34.3 66.1 %copy-start.1 = (f32[106,384]{1,0:T(8,128)}, f32[106,384]{1,0:T(8,128)S(1)}, u32[]{:S(2)}) copy-start(f32[106,384]{1,0:T(8,128)S(1)} %get-tuple-element.9) | copy-start | bytes 488452
  49.6 73.2 %all-gather.4.cloned.1.call-start = ((), (), s32[]{:S(2)}) async-start(), calls=%async_computation | async-start | bytes 4737024 | tf_op jit(solution)/shard_map/all_gather | solution.py:65
  107.4 2.8 %copy-start.7 = (s32[1,2]{1,0:T(1,128)S(1)}, s32[1,2]{1,0:T(1,128)}, u32[]{:S(2)}) copy-start(s32[1,2]{1,0:T(1,128)} %param.15) | copy-start | bytes 28
Sparse Core Ops, SparseCore 0:
  49.7 46.1 all-gather.5
  110.3 12.4 all-gather.3
where the time goes:
time: 138 us; the launch traced here: 137 us
  waiting for transfers between devices  58.9 us (43%)
  blocking collectives  35.6 us (26%)
  between operations  15.7 us (11%)
  local copies, waits for them, and re-layouts  13.4 us (10%)
  other arithmetic  5.28 us (4%)
  matrix products  4.87 us (4%)
  starting transfers between devices  3.31 us (2%)
    all_gather x1, waiting for transfers between devices, shards(): gathered = lax.all_gather(column_block, ('dp', 'crop'), axis=0, tiled=True)  46.3 us
    unnamed x1, blocking collectives  20.4 us
    all_gather x1, blocking collectives, shards(): column_block = lax.all_gather(teacher_new, 'fsdp', axis=1, tiled=True)  15.2 us
    all_gather x1, waiting for transfers between devices, shards(): both = lax.all_gather(own_tokens[:, None], 'crop', axis=1, tiled=True)  12.6 us
    unnamed x21, local copies, waits for them, and re-layouts  5.6 us
    dot_general x1, matrix products, embed(): jnp.dot(flat_patches, weight, precision=lax.Precision.HIGHEST, preferred_...  4.87 us
    slice x1, local copies, waits for them, and re-layouts, shards(): both[:, 0:1]  4.05 us
    unnamed x1, starting transfers between devices  3.23 us
  transfers between devices with their start and end apart: 3, of which 2 were waited for; matrix products, arithmetic and copies ran while one was open for 0% of the time, Pallas kernels for 0%

commit v1 on v0

--- a/solution.py
+++ b/solution.py
@@ -1,8 +1,11 @@
+import functools
 import math
 
 import jax
 import jax.numpy as jnp
 from jax import lax
+from jax.experimental import pallas as pl
+from jax.experimental.pallas import tpu as pltpu
 from jax.sharding import PartitionSpec as P
 
 beta_one = 0.9
@@ -54,6 +57,243 @@
     return centered * lax.rsqrt(variance + norm_epsilon) * extras[2] + extras[3]
 
 
+LEVELS = 32767.0
+CODES = 256.0
+MESH = pl.DeviceIdType.MESH
+
+
+def padded_rows(rows):
+    return -(-(rows + 1) // 16) * 16
+
+
+def diagonal(count, width):
+    first = lax.broadcasted_iota(jnp.int32, (count, width), 0)
+    second = lax.broadcasted_iota(jnp.int32, (count, width), 1)
+    return first == second
+
+
+def encode(value, rows):
+    count, width = value.shape
+    row_index = lax.broadcasted_iota(jnp.int32, (count, width), 0)
+    value = jnp.where(row_index < rows, value, 0.0)
+    top = jnp.maximum(jnp.max(jnp.abs(value), axis=1, keepdims=True), 1e-30)
+    code = jnp.ceil(jnp.log2(top) * CODES + 0.01)
+    scaled = value * (jnp.exp2(code * (-1.0 / CODES)) * LEVELS)
+    code_row = jnp.sum(
+        jnp.where(diagonal(count, width), jnp.broadcast_to(code, (count, width)), 0.0),
+        axis=0,
+        keepdims=True,
+    )
+    out = jnp.where(row_index == rows, jnp.broadcast_to(code_row, (count, width)), scaled)
+    out = jnp.clip(jnp.round(out), -LEVELS, LEVELS)
+    return out.astype(jnp.int32).astype(jnp.int16)
+
+
+def decode(block, rows):
+    count, width = block.shape
+    value = block.astype(jnp.int32).astype(jnp.float32)
+    code_row = value[rows : rows + 1]
+    code = jnp.sum(
+        jnp.where(diagonal(count, width), jnp.broadcast_to(code_row, (count, width)), 0.0),
+        axis=1,
+        keepdims=True,
+    )
+    return value * (jnp.exp2(code * (1.0 / CODES)) * (1.0 / LEVELS))
+
+
+def refresh_kernel(
+    sizes, grad_ref, pixel_ref, student_ref, teacher_ref, moment1_ref, moment2_ref, fix_ref,
+    gradient_ref, table_ref, other_ref,
+    out_ref, in_ref, space_ref, out_sem, in_sem, pix_sem, go_sem, come_sem,
+):
+    DP, F, C = sizes
+    rows = student_ref.shape[0]
+    d, f, c = lax.axis_index("dp"), lax.axis_index("fsdp"), lax.axis_index("crop")
+    me = d * C + c
+    N = DP * C
+
+    barrier = pltpu.get_barrier_semaphore()
+    for r in range(1, N):
+        to = lax.rem(me + r, N)
+        pl.semaphore_signal(barrier, inc=1, device_id={"dp": to // C, "crop": lax.rem(to, C)}, device_id_type=MESH)
+    for r in range(1, F):
+        pl.semaphore_signal(barrier, inc=1, device_id={"fsdp": lax.rem(f + r, F)}, device_id_type=MESH)
+
+    space_ref[...] = jnp.zeros_like(space_ref)
+    for j in range(N):
+        space_ref[0:rows] = grad_ref[0, j * rows : (j + 1) * rows]
+        out_ref[j] = encode(space_ref[...], rows)
+    pl.semaphore_wait(barrier, N - 1 + F - 1)
+
+    sends = []
+    for r in range(1, N):
+        to = lax.rem(me + r, N)
+        copy = pltpu.make_async_remote_copy(
+            src_ref=out_ref.at[to], dst_ref=in_ref.at[me],
+            send_sem=out_sem.at[r], recv_sem=in_sem.at[me],
+            device_id={"dp": to // C, "crop": lax.rem(to, C)}, device_id_type=MESH,
+        )
+        copy.start()
+        sends.append(copy)
+    pixel_copy = pltpu.make_async_remote_copy(
+        src_ref=pixel_ref, dst_ref=other_ref, send_sem=pix_sem.at[0], recv_sem=pix_sem.at[1],
+        device_id={"crop": lax.rem(c + 1, C)}, device_id_type=MESH,
+    )
+    pixel_copy.start()
+
+    total = decode(out_ref[me], rows)
+    for r in range(1, N):
+        source = lax.rem(me + r, N)
+        pltpu.make_async_copy(in_ref.at[source], in_ref.at[source], in_sem.at[source]).wait()
+        total = total + decode(in_ref[source], rows)
+    gradient = total[0:rows]
+    gradient_ref[...] = gradient
+
+    student = student_ref[...]
+    first_moment = beta_one * moment1_ref[...] + (1.0 - beta_one) * gradient
+    second_moment = beta_two * moment2_ref[...] + (1.0 - beta_two) * gradient * gradient
+    update = (
+        first_moment / fix_ref[0] / (jnp.sqrt(second_moment / fix_ref[1]) + adam_epsilon)
+        + weight_decay * student
+    )
+    student_new = student - learn_rate * update
+    space_ref[0:rows] = fix_ref[2] * teacher_ref[...] + (1.0 - fix_ref[2]) * student_new
+    table_ref[f, d, c] = encode(space_ref[...], rows)
+
+    def pass_on(at, to):
+        number = len(sends) - (N - 1)
+        copy = pltpu.make_async_remote_copy(
+            src_ref=table_ref.at[at], dst_ref=table_ref.at[at],
+            send_sem=go_sem.at[number], recv_sem=come_sem.at[at],
+            device_id=to, device_id_type=MESH,
+        )
+        copy.start()
+        sends.append(copy)
+
+    def arrive(at):
+        pltpu.make_async_copy(table_ref.at[at], table_ref.at[at], come_sem.at[at]).wait()
+
+    partner = lax.rem(c + 1, C)
+    for q in range(F):
+        at = (lax.rem(f + q, F), d, c)
+        if q == 0:
+            for r in range(1, F):
+                pass_on(at, {"fsdp": lax.rem(f + r, F)})
+        else:
+            arrive(at)
+        for r in range(1, DP):
+            pass_on(at, {"dp": lax.rem(d + r, DP)})
+        pass_on(at, {"crop": partner})
+    for q in range(F):
+        for r in range(1, DP):
+            at = (lax.rem(f + q, F), lax.rem(d + r, DP), c)
+            arrive(at)
+            pass_on(at, {"crop": partner})
+    for q in range(F):
+        for r in range(DP):
+            arrive((lax.rem(f + q, F), lax.rem(d + r, DP), partner))
+    pixel_copy.wait()
+    for copy in sends:
+        copy.wait_send()
+
+
+def tokens_kernel(sizes, table_ref, own_ref, other_ref, pick_ref, tokens_ref, flat_ref, high_ref, low_ref, x_ref):
+    DP, F, C = sizes
+    patch_count, pix_size = own_ref.shape
+    columns = table_ref.shape[-1]
+    width = flat_ref.shape[1]
+    rows = flat_ref.shape[0] // (DP * C)
+    base = pix_size + patch_count
+
+    @pl.when(pl.program_id(0) == 0)
+    def _():
+        for i in range(F):
+            for j in range(DP * C):
+                block = decode(table_ref[i, j // C, j % C], rows)
+                flat_ref[j * rows : (j + 1) * rows, i * columns : (i + 1) * columns] = block[0:rows]
+        weight = flat_ref[0:pix_size]
+        high = weight.astype(jnp.bfloat16)
+        high_ref[...] = high
+        low_ref[...] = (weight - high.astype(jnp.float32)).astype(jnp.bfloat16)
+        flat_ref[pix_size:base] = flat_ref[pix_size:base] + flat_ref[base + 1 : base + 2]
+
+    gain, shift = flat_ref[base + 2 : base + 3], flat_ref[base + 3 : base + 4]
+
+    def normed(x):
+        average = jnp.mean(x, axis=-1, keepdims=True)
+        centered = x - average
+        variance = jnp.mean(centered * centered, axis=-1, keepdims=True)
+        return centered * lax.rsqrt(variance + norm_epsilon) * gain + shift
+
+    pixels = jnp.where(pick_ref[pl.program_id(0)] == 1, own_ref[...], other_ref[...])
+    for i in range(F):
+        part = slice(i * columns, (i + 1) * columns)
+        x_ref[:, part] = (
+            jnp.dot(pixels, high_ref[:, part], preferred_element_type=jnp.float32)
+            + jnp.dot(pixels, low_ref[:, part], preferred_element_type=jnp.float32)
+            + flat_ref[pix_size:base, part]
+        )
+    tokens_ref[0, 0, 0:1] = normed(flat_ref[base : base + 1])
+    tokens_ref[0, 0, 1:] = normed(x_ref[...])
+
+
+def kernels(grad_parts, student, teacher, moment1, moment2, step_count, pixels, assign, sizes):
+    DP, F, C = sizes
+    rows, columns = student.shape
+    spare = padded_rows(rows)
+    step_value = step_count[0].astype(jnp.float32)
+    fixes = jnp.stack(
+        [
+            1.0 - jnp.power(jnp.float32(beta_one), step_value),
+            1.0 - jnp.power(jnp.float32(beta_two), step_value),
+            1.0 - (1.0 - momentum_base) * (jnp.cos(math.pi * step_value / plan_length) + 1.0) / 2.0,
+        ]
+    )
+    own = pixels[0, 0]
+    here = pl.BlockSpec(memory_space=pltpu.VMEM)
+    scalars = pl.BlockSpec(memory_space=pltpu.SMEM)
+    count = DP * C
+    gradient, table, other = pl.pallas_call(
+        functools.partial(refresh_kernel, sizes),
+        out_shape=(
+            jax.ShapeDtypeStruct((rows, columns), jnp.float32),
+            jax.ShapeDtypeStruct((F, DP, C, spare, columns), jnp.int16),
+            jax.ShapeDtypeStruct(own.shape, own.dtype),
+        ),
+        in_specs=[here] * 6 + [scalars],
+        out_specs=(here,) * 3,
+        scratch_shapes=[
+            pltpu.VMEM((count, spare, columns), jnp.int16),
+            pltpu.VMEM((count, spare, columns), jnp.int16),
+            pltpu.VMEM((spare, columns), jnp.float32),
+            pltpu.SemaphoreType.DMA((count,)),
+            pltpu.SemaphoreType.DMA((count,)),
+            pltpu.SemaphoreType.DMA((2,)),
+            pltpu.SemaphoreType.DMA((F - 1 + F * DP + F * (DP - 1),)),
+            pltpu.SemaphoreType.DMA((F, DP, C)),
+        ],
+        compiler_params=pltpu.CompilerParams(collective_id=0, has_side_effects=True),
+    )(grad_parts, own, student, teacher, moment1, moment2, fixes)
+    results = optimize(gradient, student, teacher, moment1, moment2, step_count)
+    patch_count, pix_size = own.shape
+    width = columns * F
+    picks = (assign[0] == lax.axis_index("crop")).astype(jnp.int32)
+    tokens = pl.pallas_call(
+        functools.partial(tokens_kernel, sizes),
+        grid=(C,),
+        out_shape=jax.ShapeDtypeStruct((1, C, patch_count + 1, width), jnp.float32),
+        in_specs=[here] * 3 + [scalars],
+        out_specs=pl.BlockSpec((1, 1, patch_count + 1, width), lambda k: (0, k, 0, 0)),
+        scratch_shapes=[
+            pltpu.VMEM((rows * count, width), jnp.float32),
+            pltpu.VMEM((pix_size, width), jnp.bfloat16),
+            pltpu.VMEM((pix_size, width), jnp.bfloat16),
+            pltpu.VMEM((patch_count, width), jnp.float32),
+        ],
+    )(table, own, other, picks)
+    return (*results, tokens)
+
+
 def shards(grad_parts, student, teacher, moment1, moment2, step_count, pixels, assign):
     gradient = lax.psum_scatter(grad_parts[0], ("dp", "crop"), scatter_dimension=0, tiled=True)
     student_new, first_moment, second_moment, teacher_new, update = optimize(
@@ -78,8 +318,21 @@
         P(("dp", "fsdp"), "crop", None, None),
         P(("dp", "fsdp"), None),
     )
+    sizes = (mesh.shape["dp"], mesh.shape["fsdp"], mesh.shape["crop"])
+
+    def run(*args):
+        grad_parts, student, pixels = args[0], args[1], args[6]
+        fits = (
+            student.shape[1] % 128 == 0
+            and padded_rows(student.shape[0]) <= student.shape[1]
+            and pixels.shape[:2] == (1, 1)
+            and grad_parts.shape[0] == 1
+            and sizes[2] == 2
+        )
+        return kernels(*args, sizes) if fits else shards(*args)
+
     return jax.shard_map(
-        shards,
+        run,
         mesh=mesh,
         in_specs=placed,
         out_specs=(

time: 138 us -> 63.8 us (0.46)
  waiting for transfers between devices: 58.9 us -> 0 us
  Pallas kernels: 0 us -> 50.2 us
  blocking collectives: 35.6 us -> 0 us
  between operations: 15.7 us -> 1.46 us
  local copies, waits for them, and re-layouts: 13.4 us -> 7.88 us
  matrix products: 4.87 us -> 0 us
  starting transfers between devices: 3.31 us -> 0 us
    all_gather x2 -> x0, waiting for transfers between devices: 58.9 us -> none  [the longest x1 46.3 us: shards(): gathered = lax.all_gather(column_block, ('dp', 'crop'), axis=0, tiled=True)]
    pallas_call x0 -> x2, Pallas kernels: none -> 50.2 us  [the longest x1 40.8 us: kernels(): pl.pallas_call(functools.partial(refresh_kernel, sizes), out_shape=(jax.S...]
    unnamed x1 -> x0, blocking collectives: 20.4 us -> none
    all_gather x1 -> x0, blocking collectives: 15.2 us -> none  [shards(): column_block = lax.all_gather(teacher_new, 'fsdp', axis=1, tiled=True)]
    slice x2 -> x0, local copies, waits for them, and re-layouts: 5.06 us -> none  [the longest x1 4.05 us: shards(): both[:, 0:1]]
    dot_general x1 -> x0, matrix products: 4.87 us -> none  [embed(): jnp.dot(flat_patches, weight, precision=lax.Precision.HIGHEST, preferred_...]
    unnamed x1 -> x0, starting transfers between devices: 3.23 us -> none
    select_n x1 -> x0, other arithmetic: 3.22 us -> none  [shards(): jnp.where((assign == 0)[:, :, None, None], both[:, 0:1], both[:, 1:2])]
  transfers between devices with their start and end apart: 3 -> 0, of which waited for: 2 -> 0; matrix products, arithmetic and copies ran while one was open for 0% -> 0% of each run, Pallas kernels for 0% -> 0%
where the time goes in v1:
time: 63.8 us; the launch traced here: 63.5 us
  Pallas kernels  50.2 us (79%)
  local copies, waits for them, and re-layouts  7.88 us (12%)
  other arithmetic  3.98 us (6%)
  between operations  1.46 us (2%)
    pallas_call x1, Pallas kernels, kernels(): pl.pallas_call(functools.partial(refresh_kernel, sizes), out_shape=(jax.S...  40.8 us
    pallas_call x1, Pallas kernels, kernels(): pl.pallas_call(functools.partial(tokens_kernel, sizes), grid=(C,), out_sh...  9.38 us
    unnamed x2, local copies, waits for them, and re-layouts  7.88 us
    add x1, other arithmetic, optimize(): teacher_new = momentum * teacher + (1.0 - momentum) * student_new  2.23 us

profile of v1, /device:TPU:9, one launch (start us, length us, event | category | flops | bytes accessed | tf_op | source)
XLA Modules:
  0.0 63.5 jit_solution(16946461164537128051)
XLA Ops:
  1.4 1.2 %fusion.1.pick_ref = s32[2]{0:T(128)} fusion(s32[1,2]{1,0:T(1,128)} %param.15, s32[]{:T(128)S(6)} %axis_index.12), kind=kLoop, calls=%fused_computation.7 | loop fusion | flops 4 | bytes 20 | tf_op jit(solution)/shard_map/convert_element_type | solution.py:280
  2.6 0.6 pad_maximum_fusion.fix_ref
  3.2 1.9 %copy.14 = bf16[1,1,256,588]{3,2,1,0:T(8,128)(2,1)} copy(bf16[1,1,256,588]{2,3,1,0:T(8,128)(2,1)} %param.14) | data formatting | bytes 602112 | tf_op args[6]
  5.1 40.8 %shard_map.127 = (f32[106,384]{1,0:T(8,128)}, s16[4,4,2,112,384]{4,3,2,1,0:T(8,128)(2,1)}, bf16[256,588]{1,0:T(8,128)(2,1)}) custom-call(f32[1,848,384]{2,1,0:T(8,128)} %grad_ref.1, bf16[256,588]{1,0:T(8,128)(2,1)} %bitcast.6, f32[106,384]{1,0:T(8,128)} %student_ref.1, f32[106,384]{1,0:T(8,128)} %teacher_ref.1, f32[106,384]{1,0:T(8,128)} %moment1_ref.1, ...), custom_call_target="tpu_custom_call" | custom-call | tf_op jit(solution)/shard_map/pallas_call | solution.py:256
  45.9 2.2 %multiply_add_fusion = (f32[106,384]{1,0:T(8,128)}, f32[106,384]{1,0:T(8,128)}, f32[106,384]{1,0:T(8,128)}, f32[106,384]{1,0:T(8,128)}, f32[106,384]{1,0:T(8,128)}) fusion(f32[106,384]{1,0:T(8,128)} %teacher_ref.1, f32[]{:T(128)S(6)} %sub.30, f32[]{:T(128)} %bitcast.3, f32[106,384]{1,0:T(8,128)} %student_ref.1, f32[]{:T(128)} %bitcast.2, f32[]{:T(128)} %bitcast.1, ...), kind=kLoop, calls=%fused_computation.2 | loop fusion | flops 732672 | bytes 1628176 | tf_op jit(solution)/shard_map/add | solution.py:35
  48.1 9.4 %shard_map.128 = f32[1,2,257,1536]{3,2,1,0:T(8,128)} custom-call(s16[4,4,2,112,384]{4,3,2,1,0:T(8,128)(2,1)} %get-tuple-element.10.table_ref, bf16[256,588]{1,0:T(8,128)(2,1)} %bitcast.7, bf16[256,588]{1,0:T(8,128)(2,1)} %get-tuple-element.11.other_ref, s32[2]{0:T(128)} %fusion.1.pick_ref), custom_call_target="tpu_custom_call" | custom-call | tf_op jit(solution)/shard_map/pallas_call | solution.py:281
  57.5 6.0 %copy.15 = f32[1,2,257,1536]{3,1,2,0:T(2,128)} copy(f32[1,2,257,1536]{3,2,1,0:T(8,128)} %shard_map.128) | data formatting | bytes 6316032

commit v2 on v1

--- a/solution.py
+++ b/solution.py
@@ -120,21 +120,20 @@
         pl.semaphore_signal(barrier, inc=1, device_id={"fsdp": lax.rem(f + r, F)}, device_id_type=MESH)
 
     space_ref[...] = jnp.zeros_like(space_ref)
+    blocks = []
     for j in range(N):
         space_ref[0:rows] = grad_ref[0, j * rows : (j + 1) * rows]
         out_ref[j] = encode(space_ref[...], rows)
-    pl.semaphore_wait(barrier, N - 1 + F - 1)
-
+        if j == 0:
+            pl.semaphore_wait(barrier, N - 1 + F - 1)
+        copy = pltpu.make_async_remote_copy(
+            src_ref=out_ref.at[j], dst_ref=in_ref.at[me],
+            send_sem=out_sem.at[j], recv_sem=in_sem.at[me],
+            device_id={"dp": j // C, "crop": j % C}, device_id_type=MESH,
+        )
+        pl.when(j != me)(copy.start)
+        blocks.append(copy)
     sends = []
-    for r in range(1, N):
-        to = lax.rem(me + r, N)
-        copy = pltpu.make_async_remote_copy(
-            src_ref=out_ref.at[to], dst_ref=in_ref.at[me],
-            send_sem=out_sem.at[r], recv_sem=in_sem.at[me],
-            device_id={"dp": to // C, "crop": lax.rem(to, C)}, device_id_type=MESH,
-        )
-        copy.start()
-        sends.append(copy)
     pixel_copy = pltpu.make_async_remote_copy(
         src_ref=pixel_ref, dst_ref=other_ref, send_sem=pix_sem.at[0], recv_sem=pix_sem.at[1],
         device_id={"crop": lax.rem(c + 1, C)}, device_id_type=MESH,
@@ -161,7 +160,7 @@
     table_ref[f, d, c] = encode(space_ref[...], rows)
 
     def pass_on(at, to):
-        number = len(sends) - (N - 1)
+        number = len(sends)
         copy = pltpu.make_async_remote_copy(
             src_ref=table_ref.at[at], dst_ref=table_ref.at[at],
             send_sem=go_sem.at[number], recv_sem=come_sem.at[at],
@@ -174,6 +173,10 @@
         pltpu.make_async_copy(table_ref.at[at], table_ref.at[at], come_sem.at[at]).wait()
 
     partner = lax.rem(c + 1, C)
+    row, column = d // 2, lax.rem(d, 2)
+    beside = row * 2 + 1 - column
+    across = (1 - row) * 2 + column
+    corner = (1 - row) * 2 + 1 - column
     for q in range(F):
         at = (lax.rem(f + q, F), d, c)
         if q == 0:
@@ -181,41 +184,48 @@
                 pass_on(at, {"fsdp": lax.rem(f + r, F)})
         else:
             arrive(at)
-        for r in range(1, DP):
-            pass_on(at, {"dp": lax.rem(d + r, DP)})
+        pass_on(at, {"dp": beside})
+        pass_on(at, {"dp": across})
         pass_on(at, {"crop": partner})
     for q in range(F):
-        for r in range(1, DP):
-            at = (lax.rem(f + q, F), lax.rem(d + r, DP), c)
+        for near, far in ((beside, across), (across, beside)):
+            at = (lax.rem(f + q, F), near, c)
             arrive(at)
+            if (q % 2 == 0) == (near is beside):
+                pass_on(at, {"dp": far})
             pass_on(at, {"crop": partner})
+    for q in range(F):
+        at = (lax.rem(f + q, F), corner, c)
+        arrive(at)
+        pass_on(at, {"crop": partner})
     for q in range(F):
         for r in range(DP):
             arrive((lax.rem(f + q, F), lax.rem(d + r, DP), partner))
     pixel_copy.wait()
+    for j, copy in enumerate(blocks):
+        pl.when(j != me)(copy.wait_send)
     for copy in sends:
         copy.wait_send()
 
 
 def tokens_kernel(sizes, table_ref, own_ref, other_ref, pick_ref, tokens_ref, flat_ref, high_ref, low_ref, x_ref):
     DP, F, C = sizes
-    patch_count, pix_size = own_ref.shape
+    pix_size, patch_count = own_ref.shape
     columns = table_ref.shape[-1]
     width = flat_ref.shape[1]
     rows = flat_ref.shape[0] // (DP * C)
     base = pix_size + patch_count
-
-    @pl.when(pl.program_id(0) == 0)
-    def _():
-        for i in range(F):
-            for j in range(DP * C):
-                block = decode(table_ref[i, j // C, j % C], rows)
-                flat_ref[j * rows : (j + 1) * rows, i * columns : (i + 1) * columns] = block[0:rows]
-        weight = flat_ref[0:pix_size]
-        high = weight.astype(jnp.bfloat16)
-        high_ref[...] = high
-        low_ref[...] = (weight - high.astype(jnp.float32)).astype(jnp.bfloat16)
-        flat_ref[pix_size:base] = flat_ref[pix_size:base] + flat_ref[base + 1 : base + 2]
+    over = (((0,), (0,)), ((), ()))
+
+    for i in range(F):
+        for j in range(DP * C):
+            block = decode(table_ref[i, j // C, j % C], rows)
+            flat_ref[j * rows : (j + 1) * rows, i * columns : (i + 1) * columns] = block[0:rows]
+    weight = flat_ref[0:pix_size]
+    high = weight.astype(jnp.bfloat16)
+    high_ref[...] = high
+    low_ref[...] = (weight - high.astype(jnp.float32)).astype(jnp.bfloat16)
+    flat_ref[pix_size:base] = flat_ref[pix_size:base] + flat_ref[base + 1 : base + 2]
 
     gain, shift = flat_ref[base + 2 : base + 3], flat_ref[base + 3 : base + 4]
 
@@ -225,16 +235,21 @@
         variance = jnp.mean(centered * centered, axis=-1, keepdims=True)
         return centered * lax.rsqrt(variance + norm_epsilon) * gain + shift
 
-    pixels = jnp.where(pick_ref[pl.program_id(0)] == 1, own_ref[...], other_ref[...])
-    for i in range(F):
-        part = slice(i * columns, (i + 1) * columns)
-        x_ref[:, part] = (
-            jnp.dot(pixels, high_ref[:, part], preferred_element_type=jnp.float32)
-            + jnp.dot(pixels, low_ref[:, part], preferred_element_type=jnp.float32)
-            + flat_ref[pix_size:base, part]
-        )
-    tokens_ref[0, 0, 0:1] = normed(flat_ref[base : base + 1])
-    tokens_ref[0, 0, 1:] = normed(x_ref[...])
+    class_row = normed(flat_ref[base : base + 1])
+    for k in range(C):
+        pixels = jnp.where(pick_ref[0, k] == lax.axis_index("crop"), own_ref[...], other_ref[...])
+        for i in range(F):
+            part = slice(i * columns, (i + 1) * columns)
+            x_ref[:, part] = (
+                lax.dot_general(pixels, high_ref[:, part], over, preferred_element_type=jnp.float32)
+                + lax.dot_general(pixels, low_ref[:, part], over, preferred_element_type=jnp.float32)
+                + flat_ref[pix_size:base, part]
+            )
+        tokens_ref[0:1, k] = class_row
+        step = 32
+        for start in range(0, patch_count, step):
+            rows_now = normed(x_ref[start : start + step])
+            tokens_ref[start + 1 : start + 1 + step, k] = rows_now
 
 
 def kernels(grad_parts, student, teacher, moment1, moment2, step_count, pixels, assign, sizes):
@@ -249,7 +264,7 @@
             1.0 - (1.0 - momentum_base) * (jnp.cos(math.pi * step_value / plan_length) + 1.0) / 2.0,
         ]
     )
-    own = pixels[0, 0]
+    own = pixels[0, 0].T
     here = pl.BlockSpec(memory_space=pltpu.VMEM)
     scalars = pl.BlockSpec(memory_space=pltpu.SMEM)
     count = DP * C
@@ -269,29 +284,27 @@
             pltpu.SemaphoreType.DMA((count,)),
             pltpu.SemaphoreType.DMA((count,)),
             pltpu.SemaphoreType.DMA((2,)),
-            pltpu.SemaphoreType.DMA((F - 1 + F * DP + F * (DP - 1),)),
+            pltpu.SemaphoreType.DMA((F - 1 + F * 7,)),
             pltpu.SemaphoreType.DMA((F, DP, C)),
         ],
         compiler_params=pltpu.CompilerParams(collective_id=0, has_side_effects=True),
     )(grad_parts, own, student, teacher, moment1, moment2, fixes)
     results = optimize(gradient, student, teacher, moment1, moment2, step_count)
-    patch_count, pix_size = own.shape
+    pix_size, patch_count = own.shape
     width = columns * F
-    picks = (assign[0] == lax.axis_index("crop")).astype(jnp.int32)
     tokens = pl.pallas_call(
         functools.partial(tokens_kernel, sizes),
-        grid=(C,),
-        out_shape=jax.ShapeDtypeStruct((1, C, patch_count + 1, width), jnp.float32),
+        out_shape=jax.ShapeDtypeStruct((patch_count + 1, C, width), jnp.float32),
         in_specs=[here] * 3 + [scalars],
-        out_specs=pl.BlockSpec((1, 1, patch_count + 1, width), lambda k: (0, k, 0, 0)),
+        out_specs=here,
         scratch_shapes=[
             pltpu.VMEM((rows * count, width), jnp.float32),
             pltpu.VMEM((pix_size, width), jnp.bfloat16),
             pltpu.VMEM((pix_size, width), jnp.bfloat16),
             pltpu.VMEM((patch_count, width), jnp.float32),
         ],
-    )(table, own, other, picks)
-    return (*results, tokens)
+    )(table, own, other, assign)
+    return (*results, tokens.transpose(1, 0, 2)[None])
 
 
 def shards(grad_parts, student, teacher, moment1, moment2, step_count, pixels, assign):
@@ -327,6 +340,7 @@
             and padded_rows(student.shape[0]) <= student.shape[1]
             and pixels.shape[:2] == (1, 1)
             and grad_parts.shape[0] == 1
+            and sizes[0] == 4
             and sizes[2] == 2
         )
         return kernels(*args, sizes) if fits else shards(*args)

time: 63.8 us -> 52.8 us (0.83)
  local copies, waits for them, and re-layouts: 7.88 us -> 0 us
  Pallas kernels: 50.2 us -> 48.4 us
  other arithmetic: 3.98 us -> 2.82 us
    unnamed x2 -> x0, local copies, waits for them, and re-layouts: 7.88 us -> none
    pallas_call x1, Pallas kernels: 40.8 us -> 39.3 us  [kernels(): pl.pallas_call(functools.partial(refresh_kernel, sizes), out_shape=(jax.S...]
    convert_element_type x1 -> x0, other arithmetic: 1.16 us -> none  [kernels(): picks = (assign[0] == lax.axis_index('crop')).astype(jnp.int32)]
where the time goes in v2:
time: 52.8 us; the launch traced here: 52.6 us
  Pallas kernels  48.4 us (92%)
  other arithmetic  2.82 us (5%)
  between operations  1.45 us (3%)
    pallas_call x1, Pallas kernels, kernels(): pl.pallas_call(functools.partial(refresh_kernel, sizes), out_shape=(jax.S...  39.3 us
    pallas_call x1, Pallas kernels, kernels(): pl.pallas_call(functools.partial(tokens_kernel, sizes), out_shape=jax.Sha...  9.09 us
    add x1, other arithmetic, optimize(): teacher_new = momentum * teacher + (1.0 - momentum) * student_new  2.23 us

profile of v2, /device:TPU:9, one launch (start us, length us, event | category | flops | bytes accessed | tf_op | source)
XLA Modules:
  0.0 52.6 jit_solution(13375883837134313032)
XLA Ops:
  1.4 0.6 %pad_maximum_fusion.fix_ref = f32[3]{0:T(128)} fusion(f32[1]{0:T(128)} %sub.31, f32[1]{0:T(128)} %sub.25, f32[1]{0:T(128)} %sub.24), kind=kLoop, calls=%fused_computation.6 | loop fusion | flops 6 | bytes 24 | tf_op jit(solution)/shard_map/stack | solution.py:260
  2.0 39.3 %shard_map.127 = (f32[106,384]{1,0:T(8,128)}, s16[4,4,2,112,384]{4,3,2,1,0:T(8,128)(2,1)}, bf16[588,256]{1,0:T(8,128)(2,1)}) custom-call(f32[1,848,384]{2,1,0:T(8,128)} %grad_ref.1, bf16[588,256]{1,0:T(8,128)(2,1)} %bitcast.10, f32[106,384]{1,0:T(8,128)} %student_ref.1, f32[106,384]{1,0:T(8,128)} %teacher_ref.1, f32[106,384]{1,0:T(8,128)} %moment1_ref.1, ...), custom_call_target="tpu_custom_call" | custom-call | tf_op jit(solution)/shard_map/pallas_call | solution.py:271
  41.3 2.2 %multiply_add_fusion = (f32[106,384]{1,0:T(8,128)}, f32[106,384]{1,0:T(8,128)}, f32[106,384]{1,0:T(8,128)}, f32[106,384]{1,0:T(8,128)}, f32[106,384]{1,0:T(8,128)}) fusion(f32[106,384]{1,0:T(8,128)} %teacher_ref.1, f32[]{:T(128)S(6)} %sub.30, f32[]{:T(128)} %bitcast.4, f32[106,384]{1,0:T(8,128)} %student_ref.1, f32[]{:T(128)} %bitcast.3, f32[]{:T(128)} %bitcast.2, ...), kind=kLoop, calls=%fused_computation.2 | loop fusion | flops 732672 | bytes 1628176 | tf_op jit(solution)/shard_map/add | solution.py:35
  43.5 9.1 %shard_map.128 = f32[257,2,1536]{2,1,0:T(2,128)} custom-call(s16[4,4,2,112,384]{4,3,2,1,0:T(8,128)(2,1)} %get-tuple-element.10.table_ref, bf16[588,256]{1,0:T(8,128)(2,1)} %bitcast.11, bf16[588,256]{1,0:T(8,128)(2,1)} %get-tuple-element.11.other_ref, s32[1,2]{1,0:T(1,128)} %pick_ref.1), custom_call_target="tpu_custom_call" | custom-call | tf_op jit(solution)/shard_map/pallas_call | solution.py:295

commit v3 on v2

--- a/solution.py
+++ b/solution.py
@@ -66,6 +66,10 @@
     return -(-(rows + 1) // 16) * 16
 
 
+def lanes_of(count):
+    return -(-count // 128) * 128
+
+
 def diagonal(count, width):
     first = lax.broadcasted_iota(jnp.int32, (count, width), 0)
     second = lax.broadcasted_iota(jnp.int32, (count, width), 1)
@@ -79,11 +83,11 @@
     top = jnp.maximum(jnp.max(jnp.abs(value), axis=1, keepdims=True), 1e-30)
     code = jnp.ceil(jnp.log2(top) * CODES + 0.01)
     scaled = value * (jnp.exp2(code * (-1.0 / CODES)) * LEVELS)
-    code_row = jnp.sum(
-        jnp.where(diagonal(count, width), jnp.broadcast_to(code, (count, width)), 0.0),
-        axis=0,
-        keepdims=True,
-    )
+    near = jnp.where(diagonal(count, lanes_of(count)), code, 0.0)
+    code_row = jnp.sum(near, axis=0, keepdims=True)
+    if width > lanes_of(count):
+        rest = jnp.zeros((1, width - lanes_of(count)), jnp.float32)
+        code_row = jnp.concatenate([code_row, rest], axis=1)
     out = jnp.where(row_index == rows, jnp.broadcast_to(code_row, (count, width)), scaled)
     out = jnp.clip(jnp.round(out), -LEVELS, LEVELS)
     return out.astype(jnp.int32).astype(jnp.int16)
@@ -92,59 +96,72 @@
 def decode(block, rows):
     count, width = block.shape
     value = block.astype(jnp.int32).astype(jnp.float32)
-    code_row = value[rows : rows + 1]
-    code = jnp.sum(
-        jnp.where(diagonal(count, width), jnp.broadcast_to(code_row, (count, width)), 0.0),
-        axis=1,
-        keepdims=True,
-    )
+    code_row = value[rows : rows + 1, : lanes_of(count)]
+    near = jnp.where(diagonal(count, lanes_of(count)), code_row, 0.0)
+    code = jnp.sum(near, axis=1, keepdims=True)
     return value * (jnp.exp2(code * (1.0 / CODES)) * (1.0 / LEVELS))
 
 
 def refresh_kernel(
     sizes, grad_ref, pixel_ref, student_ref, teacher_ref, moment1_ref, moment2_ref, fix_ref,
     gradient_ref, table_ref, other_ref,
-    out_ref, in_ref, space_ref, out_sem, in_sem, pix_sem, go_sem, come_sem,
+    all_ref, pre_ref, out_ref, in_ref, space_ref, pair_sem, out_sem, in_sem, pix_sem, go_sem, come_sem,
 ):
     DP, F, C = sizes
     rows = student_ref.shape[0]
     d, f, c = lax.axis_index("dp"), lax.axis_index("fsdp"), lax.axis_index("crop")
-    me = d * C + c
-    N = DP * C
+    partner = lax.rem(c + 1, C)
 
     barrier = pltpu.get_barrier_semaphore()
-    for r in range(1, N):
-        to = lax.rem(me + r, N)
-        pl.semaphore_signal(barrier, inc=1, device_id={"dp": to // C, "crop": lax.rem(to, C)}, device_id_type=MESH)
+    pl.semaphore_signal(barrier, inc=1, device_id={"crop": partner}, device_id_type=MESH)
+    for r in range(1, DP):
+        pl.semaphore_signal(barrier, inc=1, device_id={"dp": lax.rem(d + r, DP)}, device_id_type=MESH)
     for r in range(1, F):
         pl.semaphore_signal(barrier, inc=1, device_id={"fsdp": lax.rem(f + r, F)}, device_id_type=MESH)
 
-    space_ref[...] = jnp.zeros_like(space_ref)
+    for b in range(DP):
+        for k in range(C):
+            j = b * C + k
+            all_ref[k, b, 0:rows] = grad_ref[0, j * rows : (j + 1) * rows]
+            all_ref[k, b, rows:] = jnp.zeros((all_ref.shape[2] - rows, all_ref.shape[3]), jnp.float32)
+    pl.semaphore_wait(barrier, DP - 1 + 1 + F - 1)
+    order = [DP - r for r in range(1, DP)] + [0]
+    sends = []
+    for r in order:
+        at = lax.rem(d + r, DP)
+        copy = pltpu.make_async_remote_copy(
+            src_ref=all_ref.at[partner, at], dst_ref=pre_ref.at[lax.rem(d + r, DP)],
+            send_sem=pair_sem.at[0, r], recv_sem=pair_sem.at[1, r],
+            device_id={"crop": partner}, device_id_type=MESH,
+        )
+        copy.start()
+        sends.append(copy)
     blocks = []
-    for j in range(N):
-        space_ref[0:rows] = grad_ref[0, j * rows : (j + 1) * rows]
-        out_ref[j] = encode(space_ref[...], rows)
-        if j == 0:
-            pl.semaphore_wait(barrier, N - 1 + F - 1)
+    total = None
+    for number, r in enumerate(order):
+        at = lax.rem(d + r, DP)
+        sends[number].wait_recv()
+        chip = all_ref[c, at] + pre_ref[at]
+        if r == 0:
+            total = chip
+            break
+        out_ref[r] = encode(chip, rows)
         copy = pltpu.make_async_remote_copy(
-            src_ref=out_ref.at[j], dst_ref=in_ref.at[me],
-            send_sem=out_sem.at[j], recv_sem=in_sem.at[me],
-            device_id={"dp": j // C, "crop": j % C}, device_id_type=MESH,
+            src_ref=out_ref.at[r], dst_ref=in_ref.at[r],
+            send_sem=out_sem.at[r], recv_sem=in_sem.at[r],
+            device_id={"dp": at}, device_id_type=MESH,
         )
-        pl.when(j != me)(copy.start)
+        copy.start()
         blocks.append(copy)
-    sends = []
     pixel_copy = pltpu.make_async_remote_copy(
         src_ref=pixel_ref, dst_ref=other_ref, send_sem=pix_sem.at[0], recv_sem=pix_sem.at[1],
         device_id={"crop": lax.rem(c + 1, C)}, device_id_type=MESH,
     )
     pixel_copy.start()
 
-    total = decode(out_ref[me], rows)
-    for r in range(1, N):
-        source = lax.rem(me + r, N)
-        pltpu.make_async_copy(in_ref.at[source], in_ref.at[source], in_sem.at[source]).wait()
-        total = total + decode(in_ref[source], rows)
+    for number, copy in enumerate(blocks):
+        copy.wait_recv()
+        total = total + decode(in_ref[order[number]], rows)
     gradient = total[0:rows]
     gradient_ref[...] = gradient
 
@@ -156,11 +173,12 @@
         + weight_decay * student
     )
     student_new = student - learn_rate * update
+    space_ref[rows:] = jnp.zeros((space_ref.shape[0] - rows, space_ref.shape[1]), jnp.float32)
     space_ref[0:rows] = fix_ref[2] * teacher_ref[...] + (1.0 - fix_ref[2]) * student_new
     table_ref[f, d, c] = encode(space_ref[...], rows)
 
     def pass_on(at, to):
-        number = len(sends)
+        number = len(sends) - DP
         copy = pltpu.make_async_remote_copy(
             src_ref=table_ref.at[at], dst_ref=table_ref.at[at],
             send_sem=go_sem.at[number], recv_sem=come_sem.at[at],
@@ -172,7 +190,6 @@
     def arrive(at):
         pltpu.make_async_copy(table_ref.at[at], table_ref.at[at], come_sem.at[at]).wait()
 
-    partner = lax.rem(c + 1, C)
     row, column = d // 2, lax.rem(d, 2)
     beside = row * 2 + 1 - column
     across = (1 - row) * 2 + column
@@ -202,14 +219,30 @@
         for r in range(DP):
             arrive((lax.rem(f + q, F), lax.rem(d + r, DP), partner))
     pixel_copy.wait()
-    for j, copy in enumerate(blocks):
-        pl.when(j != me)(copy.wait_send)
-    for copy in sends:
+    for copy in blocks + sends:
         copy.wait_send()
 
 
-def tokens_kernel(sizes, table_ref, own_ref, other_ref, pick_ref, tokens_ref, flat_ref, high_ref, low_ref, x_ref):
+def tokens_kernel(
+    sizes, table_ref, own_ref, other_ref, gradient_ref, student_ref, teacher_ref, moment1_ref, moment2_ref,
+    pick_ref, fix_ref,
+    student_out, moment1_out, moment2_out, teacher_out, update_out, tokens_ref,
+    flat_ref, high_ref, low_ref, x_ref,
+):
     DP, F, C = sizes
+    student, gradient = student_ref[...], gradient_ref[...]
+    first_moment = beta_one * moment1_ref[...] + (1.0 - beta_one) * gradient
+    second_moment = beta_two * moment2_ref[...] + (1.0 - beta_two) * gradient * gradient
+    update = (
+        first_moment / fix_ref[0] / (jnp.sqrt(second_moment / fix_ref[1]) + adam_epsilon)
+        + weight_decay * student
+    )
+    student_new = student - learn_rate * update
+    student_out[...] = student_new
+    moment1_out[...] = first_moment
+    moment2_out[...] = second_moment
+    teacher_out[...] = fix_ref[2] * teacher_ref[...] + (1.0 - fix_ref[2]) * student_new
+    update_out[...] = update
     pix_size, patch_count = own_ref.shape
     columns = table_ref.shape[-1]
     width = flat_ref.shape[1]
@@ -278,32 +311,35 @@
         in_specs=[here] * 6 + [scalars],
         out_specs=(here,) * 3,
         scratch_shapes=[
-            pltpu.VMEM((count, spare, columns), jnp.int16),
-            pltpu.VMEM((count, spare, columns), jnp.int16),
+            pltpu.VMEM((C, DP, spare, columns), jnp.float32),
+            pltpu.VMEM((DP, spare, columns), jnp.float32),
+            pltpu.VMEM((DP, spare, columns), jnp.int16),
+            pltpu.VMEM((DP, spare, columns), jnp.int16),
             pltpu.VMEM((spare, columns), jnp.float32),
-            pltpu.SemaphoreType.DMA((count,)),
-            pltpu.SemaphoreType.DMA((count,)),
+            pltpu.SemaphoreType.DMA((2, DP)),
+            pltpu.SemaphoreType.DMA((DP,)),
+            pltpu.SemaphoreType.DMA((DP,)),
             pltpu.SemaphoreType.DMA((2,)),
             pltpu.SemaphoreType.DMA((F - 1 + F * 7,)),
             pltpu.SemaphoreType.DMA((F, DP, C)),
         ],
         compiler_params=pltpu.CompilerParams(collective_id=0, has_side_effects=True),
     )(grad_parts, own, student, teacher, moment1, moment2, fixes)
-    results = optimize(gradient, student, teacher, moment1, moment2, step_count)
     pix_size, patch_count = own.shape
     width = columns * F
-    tokens = pl.pallas_call(
+    *results, tokens = pl.pallas_call(
         functools.partial(tokens_kernel, sizes),
-        out_shape=jax.ShapeDtypeStruct((patch_count + 1, C, width), jnp.float32),
-        in_specs=[here] * 3 + [scalars],
-        out_specs=here,
+        out_shape=(jax.ShapeDtypeStruct((rows, columns), jnp.float32),) * 5
+        + (jax.ShapeDtypeStruct((patch_count + 1, C, width), jnp.float32),),
+        in_specs=[here] * 8 + [scalars] * 2,
+        out_specs=(here,) * 6,
         scratch_shapes=[
             pltpu.VMEM((rows * count, width), jnp.float32),
             pltpu.VMEM((pix_size, width), jnp.bfloat16),
             pltpu.VMEM((pix_size, width), jnp.bfloat16),
             pltpu.VMEM((patch_count, width), jnp.float32),
         ],
-    )(table, own, other, assign)
+    )(table, own, other, gradient, student, teacher, moment1, moment2, assign, fixes)
     return (*results, tokens.transpose(1, 0, 2)[None])
 
 

time: 52.8 us -> 49 us (0.928)
  other arithmetic: 2.82 us -> 0.59 us
  Pallas kernels: 48.4 us -> 46.8 us
    pallas_call x1, Pallas kernels: 39.3 us -> 37 us  [kernels(): pl.pallas_call(functools.partial(refresh_kernel, sizes), out_shape=(jax.S...]
    add x1 -> x0, other arithmetic: 2.23 us -> none  [optimize(): teacher_new = momentum * teacher + (1.0 - momentum) * student_new]
    pallas_call x1, Pallas kernels: 9.09 us -> 9.73 us  [kernels(): pl.pallas_call(functools.partial(tokens_kernel, sizes), out_shape=(jax.Sh...]
where the time goes in v3:
time: 49 us; the launch traced here: 48.8 us
  Pallas kernels  46.8 us (96%)
  between operations  1.45 us (3%)
  other arithmetic  0.59 us (1%)
    pallas_call x1, Pallas kernels, kernels(): pl.pallas_call(functools.partial(refresh_kernel, sizes), out_shape=(jax.S...  37 us
    pallas_call x1, Pallas kernels, kernels(): pl.pallas_call(functools.partial(tokens_kernel, sizes), out_shape=(jax.Sh...  9.73 us

profile of v3, /device:TPU:9, one launch (start us, length us, event | category | flops | bytes accessed | tf_op | source)
XLA Modules:
  0.0 48.8 jit_solution(15208210110652886184)
XLA Ops:
  1.4 0.6 %pad_maximum_fusion.fix_ref = f32[3]{0:T(128)} fusion(f32[1]{0:T(128)S(6)} %sub.14, f32[1]{0:T(128)S(6)} %sub.12, f32[1]{0:T(128)S(6)} %sub.11), kind=kLoop, calls=%fused_computation | loop fusion | flops 6 | bytes 24 | tf_op jit(solution)/shard_map/stack | solution.py:293
  2.0 37.0 %shard_map.127 = (f32[106,384]{1,0:T(8,128)}, s16[4,4,2,112,384]{4,3,2,1,0:T(8,128)(2,1)}, bf16[588,256]{1,0:T(8,128)(2,1)}) custom-call(f32[1,848,384]{2,1,0:T(8,128)} %grad_ref.1, bf16[588,256]{1,0:T(8,128)(2,1)} %bitcast.6, f32[106,384]{1,0:T(8,128)} %student_ref.3, f32[106,384]{1,0:T(8,128)} %teacher_ref.3, f32[106,384]{1,0:T(8,128)} %moment1_ref.3, ...), custom_call_target="tpu_custom_call" | custom-call | tf_op jit(solution)/shard_map/pallas_call | solution.py:304
  39.1 9.7 %shard_map.128 = (f32[106,384]{1,0:T(8,128)}, f32[106,384]{1,0:T(8,128)}, f32[106,384]{1,0:T(8,128)}, f32[106,384]{1,0:T(8,128)}, f32[106,384]{1,0:T(8,128)}, /*index=5*/f32[257,2,1536]{2,1,0:T(2,128)}) custom-call(s16[4,4,2,112,384]{4,3,2,1,0:T(8,128)(2,1)} %get-tuple-element.15.table_ref, bf16[588,256]{1,0:T(8,128)(2,1)} %bitcast.7, ...), custom_call_target="tpu_custom_call" | custom-call | tf_op jit(solution)/shard_map/pallas_call | solution.py:330

commit v4 on v3

--- a/solution.py
+++ b/solution.py
@@ -194,30 +194,42 @@
     beside = row * 2 + 1 - column
     across = (1 - row) * 2 + column
     corner = (1 - row) * 2 + 1 - column
+    turn = 1 - 2 * (2 * f // F)
+
+    def layer(q):
+        return lax.rem(f + q * turn + F, F)
+
+    def relay(q):
+        for near, far in ((beside, across), (across, beside)):
+            at = (layer(q), near, c)
+            arrive(at)
+            if (q % 2 == 0) == (near is beside):
+                pass_on(at, {"dp": far})
+            pass_on(at, {"crop": partner})
+
     for q in range(F):
-        at = (lax.rem(f + q, F), d, c)
+        at = (layer(q), d, c)
         if q == 0:
             for r in range(1, F):
-                pass_on(at, {"fsdp": lax.rem(f + r, F)})
+                pass_on(at, {"fsdp": layer(r)})
         else:
             arrive(at)
         pass_on(at, {"dp": beside})
         pass_on(at, {"dp": across})
         pass_on(at, {"crop": partner})
+        if q == 0:
+            relay(0)
+        elif q > 1:
+            relay(q - 1)
+    if F > 1:
+        relay(F - 1)
     for q in range(F):
-        for near, far in ((beside, across), (across, beside)):
-            at = (lax.rem(f + q, F), near, c)
-            arrive(at)
-            if (q % 2 == 0) == (near is beside):
-                pass_on(at, {"dp": far})
-            pass_on(at, {"crop": partner})
-    for q in range(F):
-        at = (lax.rem(f + q, F), corner, c)
+        at = (layer(q), corner, c)
         arrive(at)
         pass_on(at, {"crop": partner})
     for q in range(F):
         for r in range(DP):
-            arrive((lax.rem(f + q, F), lax.rem(d + r, DP), partner))
+            arrive((layer(q), lax.rem(d + r, DP), partner))
     pixel_copy.wait()
     for copy in blocks + sends:
         copy.wait_send()

time: 49 us -> 49.7 us (1.014)
  the two profiles are of different devices: /device:TPU:9 before, /device:TPU:0 now
where the time goes in v4:
time: 49.7 us; the launch traced here: 49.5 us
  Pallas kernels  47.5 us (96%)
  between operations  1.45 us (3%)
  other arithmetic  0.59 us (1%)
    pallas_call x1, Pallas kernels, kernels(): pl.pallas_call(functools.partial(refresh_kernel, sizes), out_shape=(jax.S...  37.8 us
    pallas_call x1, Pallas kernels, kernels(): pl.pallas_call(functools.partial(tokens_kernel, sizes), out_shape=(jax.Sh...  9.73 us

profile of v4, /device:TPU:0, one launch (start us, length us, event | category | flops | bytes accessed | tf_op | source)
XLA Modules:
  0.0 49.5 jit_solution(3768252269266251368)
XLA Ops:
  1.4 0.6 %pad_maximum_fusion.fix_ref = f32[3]{0:T(128)} fusion(f32[1]{0:T(128)S(6)} %sub.14, f32[1]{0:T(128)S(6)} %sub.12, f32[1]{0:T(128)S(6)} %sub.11), kind=kLoop, calls=%fused_computation | loop fusion | flops 6 | bytes 24 | tf_op jit(solution)/shard_map/stack | solution.py:305
  2.0 37.8 %shard_map.127 = (f32[106,384]{1,0:T(8,128)}, s16[4,4,2,112,384]{4,3,2,1,0:T(8,128)(2,1)}, bf16[588,256]{1,0:T(8,128)(2,1)}) custom-call(f32[1,848,384]{2,1,0:T(8,128)} %grad_ref.1, bf16[588,256]{1,0:T(8,128)(2,1)} %bitcast.6, f32[106,384]{1,0:T(8,128)} %student_ref.3, f32[106,384]{1,0:T(8,128)} %teacher_ref.3, f32[106,384]{1,0:T(8,128)} %moment1_ref.3, ...), custom_call_target="tpu_custom_call" | custom-call | tf_op jit(solution)/shard_map/pallas_call | solution.py:316
  39.8 9.7 %shard_map.128 = (f32[106,384]{1,0:T(8,128)}, f32[106,384]{1,0:T(8,128)}, f32[106,384]{1,0:T(8,128)}, f32[106,384]{1,0:T(8,128)}, f32[106,384]{1,0:T(8,128)}, /*index=5*/f32[257,2,1536]{2,1,0:T(2,128)}) custom-call(s16[4,4,2,112,384]{4,3,2,1,0:T(8,128)(2,1)} %get-tuple-element.15.table_ref, bf16[588,256]{1,0:T(8,128)(2,1)} %bitcast.7, ...), custom_call_target="tpu_custom_call" | custom-call | tf_op jit(solution)/shard_map/pallas_call | solution.py:342
